TPU v7x, 32 devices: a whole 2x2x4 slice. The times are simulated.
32 devices in a mesh: cplx: 4 (over y, core), dap: 8 (over z, x).
Axes of the slice: x: 2, y: 2, z: 4, core: 2. Of those that a mesh axis runs over, the one named last changes fastest.
Arguments:
- alignment_features: bfloat16 [64, 64, 256], P(('cplx', 'dap')), parts along dimension 0, may hold values from -6 to 6
- couple_features: bfloat16 [256, 64, 128], P(('cplx', 'dap')), parts along dimension 0, may hold values from -6 to 6
- alignment_presence: int32 [64, 64], P('cplx'), parts along dimension 0, may hold values 0 or 1
- amino_presence: int32 [256], P('cplx'), parts along dimension 0, may hold values 0 or 1
- strand_identity: int32 [256], P('cplx'), parts along dimension 0, may hold values from 0 to 3, never falling along the last dimension, each value on 1 to 32 neighbouring positions
- strand_couple_embedding: float32 [2, 128], replicated, may hold values from -4 to 4
- fourfold_input_matrix: bfloat16 [256, 1024], replicated, may hold values from -0.375 to 0.375
- heads_merge_matrix: bfloat16 [256, 256], replicated, may hold values from -1.5 to 1.5
- couple_logit_matrix: bfloat16 [128, 8], replicated, may hold values from -30 to 30
- twin_factor_matrix: bfloat16 [256, 64], replicated, may hold values from -0.375 to 0.375
- tensor_reduce_matrix: bfloat16 [1024, 128], replicated, may hold values from -0.75 to 0.75
Outputs:
- alignment_mixed: bfloat16 [64, 64, 256], P(('cplx', 'dap')), parts along dimension 0
- couple_refreshed: bfloat16 [256, 64, 128], P(('cplx', 'dap')), parts along dimension 0
There are 4 independent parts, one for each index of `cplx`. A program takes and returns all parts, laid end to end along the dimension named above; an argument that names none is the same for every part. Nothing has to cross between parts.
All inputs are finite; a program needn't handle non-finite values.
Results may differ from a plain program's by a relative error of at most 0.0075.
The roundings to bfloat16 on the way count: a program that leaves them out, or rounds other values in their place, can miss the bound.
Values may be sent and summed in bfloat16 or wider, within the bound.
No kernel may reach another device: no remote copies, remote signals or barrier semaphores. Data moves between devices by JAX's collectives and lax.ppermute only.
A program may use at most 64 MiB of HBM per device.

v0:
```python
import jax
import jax.numpy as jnp
from jax import lax
from jax.sharding import PartitionSpec as P

EPS = 1e-05


def standardize_features(x):
    x = x.astype(jnp.float32)
    center = x - jnp.mean(x, axis=-1, keepdims=True)
    spread = jnp.mean(center * center, axis=-1, keepdims=True)
    return center * lax.rsqrt(spread + EPS)


def on_device(
    alignment_features,
    couple_features,
    alignment_presence,
    amino_presence,
    strand_identity,
    strand_couple_embedding,
    fourfold_input_matrix,
    heads_merge_matrix,
    couple_logit_matrix,
    twin_factor_matrix,
    tensor_reduce_matrix,
):
    res_here = couple_features.shape[0]
    every_amino_line = couple_features.shape[1]
    device_aligned_lines = alignment_features.shape[0]
    width = twin_factor_matrix.shape[1] // 2
    head_count = couple_logit_matrix.shape[1]
    head_size = heads_merge_matrix.shape[0] // head_count
    position = lax.axis_index("dap")
    res_start = position * res_here
    seq_start = position * device_aligned_lines
    chain_here = lax.dynamic_slice_in_dim(strand_identity, res_start, res_here)
    same = (chain_here[:, None] == strand_identity[None, :]).astype(jnp.float32)[..., None]
    z_in = (
        couple_features.astype(jnp.float32)
        + (1.0 - same) * strand_couple_embedding[0]
        + same * strand_couple_embedding[1]
    )
    pair_ln = standardize_features(z_in).astype(jnp.bfloat16)
    bias_here = jnp.einsum(
        "ijc,ch->hij", pair_ln, couple_logit_matrix, preferred_element_type=jnp.float32
    ).astype(jnp.bfloat16)
    bias_all = lax.all_gather(bias_here, "dap", axis=1, tiled=True)
    presence_numeric = alignment_presence.astype(jnp.float32)
    mask_rows = lax.dynamic_slice_in_dim(presence_numeric, seq_start, device_aligned_lines, 0)
    standardized_alignment = standardize_features(alignment_features).astype(jnp.bfloat16)
    mapped_lines = jnp.dot(
        standardized_alignment.reshape(
            device_aligned_lines * every_amino_line, alignment_features.shape[2]
        ),
        fourfold_input_matrix,
        preferred_element_type=jnp.float32,
    )
    mapped_lines = mapped_lines.reshape(
        device_aligned_lines, every_amino_line, 4, head_count, head_size
    )
    asking_vectors = (mapped_lines[:, :, 0] * head_size ** (-0.5)).astype(jnp.bfloat16)
    target_vectors = mapped_lines[:, :, 1].astype(jnp.bfloat16)
    content_vectors = mapped_lines[:, :, 2].astype(jnp.bfloat16)
    sigmoid_factors = jax.nn.sigmoid(mapped_lines[:, :, 3])
    scores = jnp.einsum(
        "sihd,sjhd->shij", asking_vectors, target_vectors, preferred_element_type=jnp.float32
    )
    scores = (
        scores
        + bias_all.astype(jnp.float32)[None]
        + ((mask_rows - 1.0) * 1000000000.0)[:, None, None, :]
    )
    weights = jax.nn.softmax(scores, axis=-1).astype(jnp.bfloat16)
    context = jnp.einsum(
        "shij,sjhd->sihd", weights, content_vectors, preferred_element_type=jnp.float32
    )
    gated_values = (
        (sigmoid_factors * context)
        .astype(jnp.bfloat16)
        .reshape(device_aligned_lines * every_amino_line, head_count * head_size)
    )
    offset_lines = jnp.dot(
        gated_values, heads_merge_matrix, preferred_element_type=jnp.float32
    ).reshape(alignment_features.shape)
    alignment_mixed = (alignment_features.astype(jnp.float32) + offset_lines).astype(jnp.bfloat16)
    mask_cols = lax.dynamic_slice_in_dim(presence_numeric, res_start, res_here, 1)
    count = jnp.dot(mask_cols.T, presence_numeric, precision=lax.Precision.HIGHEST) + 1.0
    rows_ln = standardize_features(alignment_mixed).astype(jnp.bfloat16)
    twin_factor_features = jnp.einsum(
        "sjm,mk->jsk", rows_ln, twin_factor_matrix, preferred_element_type=jnp.float32
    )
    mask_t = mask_rows.T[..., None]
    left_rows = (
        (twin_factor_features[:, :, :width] * mask_t)
        .astype(jnp.bfloat16)
        .reshape(every_amino_line, device_aligned_lines * width)
    )
    right_rows = (
        (twin_factor_features[:, :, width:] * mask_t)
        .astype(jnp.bfloat16)
        .reshape(every_amino_line, device_aligned_lines * width)
    )
    left_full = lax.all_to_all(left_rows, "dap", split_axis=0, concat_axis=1, tiled=True)
    piece = lax.all_gather(right_rows, "dap", axis=1, tiled=True)
    columns = piece.shape[1]
    left_part = left_full.reshape(res_here, columns // width, width)
    right_part = piece.reshape(every_amino_line, columns // width, width)
    outer = jnp.einsum("isc,jse->ijce", left_part, right_part, preferred_element_type=jnp.float32)
    outer = outer.astype(jnp.bfloat16).reshape(res_here, every_amino_line, width * width)
    update = (
        jnp.einsum("ijk,kz->ijz", outer, tensor_reduce_matrix, preferred_element_type=jnp.float32)
        / count[..., None]
    )
    resf = amino_presence.astype(jnp.float32)
    res_local = lax.dynamic_slice_in_dim(resf, res_start, res_here)
    pair_mask = res_local[:, None] * resf[None, :]
    couple_refreshed = (z_in + pair_mask[..., None] * update).astype(jnp.bfloat16)
    return (alignment_mixed, couple_refreshed)


def solution(mesh):
    in_specs = (
        P(("cplx", "dap"), None, None),
        P(("cplx", "dap"), None, None),
        P("cplx", None),
        P("cplx"),
        P("cplx"),
        P(),
        P(),
        P(),
        P(),
        P(),
        P(),
    )
    out_specs = (P(("cplx", "dap"), None, None), P(("cplx", "dap"), None, None))
    return jax.shard_map(
        on_device, mesh=mesh, in_specs=in_specs, out_specs=out_specs, check_vma=False
    )
```

profile of v0, /device:TPU:0, one launch (start us, length us, event | category | flops | bytes accessed | tf_op | source)
XLA Modules:
  0.0 88.1 jit_solution(13455693065240458379)
XLA Ops:
  0.7 0.8 dynamic_slice.12
  1.4 0.7 broadcast_subtract_fusion
  2.2 0.7 compare_convert_fusion
  2.9 0.9 %convert_reduce_fusion = f32[2,64]{1,0:T(2,128)S(1)} fusion(bf16[2,64,256]{2,1,0:T(8,128)(2,1)} %param.11), kind=kLoop, calls=%fused_computation.35 | loop fusion | flops 65408 | bytes 66048 | tf_op jit(solution)/shard_map/reduce_sum | solution.py:11
  3.8 1.0 %fusion.24 = f32[2,64]{1,0:T(2,128)S(1)} fusion(bf16[2,64,256]{2,1,0:T(8,128)(2,1)} %param.11, f32[2,64]{1,0:T(2,128)S(1)} %broadcast_multiply_fusion.3), kind=kLoop, calls=%fused_computation.42 | loop fusion | flops 130944 | bytes 66560 | tf_op jit(solution)/shard_map/reduce_sum | solution.py:12
  4.9 0.8 slice_bitcast_fusion.5
  5.6 1.2 %fusion.19 = f32[8,64]{1,0:T(8,128)S(1)} fusion(bf16[8,64,128]{2,1,0:T(8,128)(2,1)} %param.12, f32[128]{0:T(128)S(1)} %get-tuple-element.7, f32[8,64]{1,0:T(8,128)S(1)} %compare_convert_fusion, f32[128]{0:T(128)S(1)} %get-tuple-element.6, f32[8,64]{1,0:T(8,128)S(1)} %broadcast_subtract_fusion), kind=kLoop, calls=%fused_computation.33 | loop fusion | flops 392704 | bytes 138240 | tf_op jit(solution)/shard_map/reduce_sum | solution.py:11
  6.9 1.3 %multiply_reduce_fusion = f32[8,64]{1,0:T(8,128)S(1)} fusion(bf16[8,64,128]{2,1,0:T(8,128)(2,1)} %param.12, f32[8,64]{1,0:T(8,128)S(1)} %broadcast_multiply_fusion.1, f32[128]{0:T(128)S(1)} %get-tuple-element.7, f32[8,64]{1,0:T(8,128)S(1)} %compare_convert_fusion, f32[128]{0:T(128)S(1)} %get-tuple-element.6, f32[8,64]{1,0:T(8,128)S(1)} %broadcast_subtract_fusion), kind=kLoop, calls=%fused_computation.30 | loop fusion | flops 523776 | bytes 140288 | tf_op jit(solution)/shard_map/reduce_sum | solution.py:12
  8.2 0.7 convert_element_type.94
  8.9 1.4 %fusion.10 = bf16[8,8,64]{2,0,1:T(8,128)(2,1)S(1)} fusion(bf16[8,64,128]{2,1,0:T(8,128)(2,1)} %param.12, f32[8,64]{1,0:T(8,128)S(1)} %add_rsqrt_fusion, f32[8,64]{1,0:T(8,128)S(1)} %broadcast_multiply_fusion.1, f32[128]{0:T(128)S(1)} %get-tuple-element.7, f32[8,64]{1,0:T(8,128)S(1)} %compare_convert_fusion, f32[128]{0:T(128)S(1)} %get-tuple-element.6, ...), kind=kOutput, calls=%fused_computation.17 | convolution fusion | flops 1576960 | bytes 150528 | tf_op jit(solution)/shard_map/ijc,ch->hij/dot_general | solution.py:46
  10.2 32.3 %all_gather.6 = bf16[8,64,64]{2,0,1:T(8,128)(2,1)S(1)} all-gather(bf16[8,8,64]{2,0,1:T(8,128)(2,1)S(1)} %fusion.10), channel_id=1, replica_groups=mesh['cplx'=4,'dap'=8] {'dap'}, dimensions={1}, use_global_device_ids=true | all-gather | bytes 73728 | tf_op jit(solution)/shard_map/all_gather | solution.py:49
  42.7 1.2 %copy.27 = bf16[256,1024]{0,1:T(8,128)(2,1)S(1)} copy(bf16[256,1024]{1,0:T(8,128)(2,1)} %param.17) | data formatting | bytes 1048576 | tf_op args[6]
  44.0 0.4 fusion.49
  44.4 0.3 fusion.3
  44.9 0.2 fusion.7
  45.1 0.5 copy-done.4
  45.6 0.3 convert_reduce_fusion.1
  46.5 0.7 reshape.178
  47.2 5.5 %all-to-all-start = ((bf16[8,2,256]{2,1,0:T(2,128)(2,1)}), bf16[8,2,256]{2,1,0:T(2,128)(2,1)S(1)}, u32[]{:S(2)}, u32[]{:S(2)}) async-start(bf16[8,2,256]{2,1,0:T(2,128)(2,1)} %reshape.178), calls=%async_computation | async-start | bytes 16384 | tf_op jit(solution)/shard_map/all_to_all | solution.py:105
  52.7 0.3 convolution_add_fusion.2
  53.1 31.1 %all_gather.7 = bf16[64,512]{0,1:T(8,128)(2,1)S(1)} all-gather(bf16[64,64]{0,1:T(8,128)(2,1)S(1)} %bitcast.75), channel_id=1, replica_groups=mesh['cplx'=4,'dap'=8] {'dap'}, dimensions={1}, use_global_device_ids=true | all-gather | bytes 73728 | tf_op jit(solution)/shard_map/all_gather | solution.py:106
  84.4 0.7 convert_bitcast_fusion
  85.1 1.4 %copy.34 = bf16[8,64,32,32]{1,3,2,0:T(8,128)(2,1)S(1)} copy(bf16[8,64,32,32]{1,2,0,3:T(8,128)(2,1)S(1)} %convert_bitcast_fusion) | data formatting | bytes 2097152 | tf_op jit(solution)/shard_map/convert_element_type | solution.py:111
  86.5 1.6 %fusion.8 = bf16[8,64,128]{2,1,0:T(8,128)(2,1)} fusion(bf16[8,64,1024]{1,2,0:T(8,128)(2,1)S(1)} %bitcast.72, bf16[1024,128]{1,0:T(8,128)(2,1)S(1)} %copy-done, bf16[8,64,128]{2,1,0:T(8,128)(2,1)S(1)} %copy-done.2, f32[8,64]{1,0:T(8,128)S(1)} %convolution_add_fusion.2, f32[8,64]{1,0:T(8,128)S(1)} %broadcast_multiply_fusion, f32[128]{0:T(128)S(1)} %get-tuple-element.7, ...), kind=kOutput, calls=%fused_computation.12 | convolution fusion | flops 134807552 | bytes 1582080 | tf_op jit(solution)/shard_map/ijk,kz->ijz/dot_general | solution.py:113
  (34 shorter events, 1.3 us)
Async XLA Ops:
  0.6 85.9 %copy-start = (bf16[1024,128]{1,0:T(8,128)(2,1)S(1)}, bf16[1024,128]{1,0:T(8,128)(2,1)}, u32[]{:S(2)}) copy-start(bf16[1024,128]{1,0:T(8,128)(2,1)} %param.21) | copy-start | bytes 786436
  0.6 43.3 %copy-start.1 = (bf16[2,64,256]{2,1,0:T(8,128)(2,1)S(1)}, bf16[2,64,256]{2,1,0:T(8,128)(2,1)}, u32[]{:S(2)}) copy-start(bf16[2,64,256]{2,1,0:T(8,128)(2,1)} %param.11) | copy-start | bytes 196612
  44.7 0.9 %copy-start.4 = (bf16[256,256]{1,0:T(8,128)(2,1)S(1)}, bf16[256,256]{1,0:T(8,128)(2,1)}, u32[]{:S(2)}) copy-start(bf16[256,256]{1,0:T(8,128)(2,1)} %param.18) | copy-start | bytes 393220
  44.8 1.2 %copy-start.5 = (bf16[256,64]{0,1:T(8,128)(2,1)S(1)}, bf16[256,64]{0,1:T(8,128)(2,1)}, u32[]{:S(2)}) copy-start(bf16[256,64]{0,1:T(8,128)(2,1)} %param.20) | copy-start | bytes 98308
  44.8 8.1 %copy-start.6 = (s32[64]{0:T(128)S(1)}, s32[64]{0:T(128)}, u32[]{:S(2)}) copy-start(s32[64]{0:T(128)} %param.14) | copy-start | bytes 772
  45.9 40.6 %copy-start.3 = (bf16[2,64,256]{2,1,0:T(8,128)(2,1)}, bf16[2,64,256]{2,1,0:T(8,128)(2,1)S(1)}, u32[]{:S(2)}) copy-start(bf16[2,64,256]{2,1,0:T(8,128)(2,1)S(1)} %get-tuple-element.11) | copy-start | bytes 196612
  47.2 37.0 %all-to-all-start = ((bf16[8,2,256]{2,1,0:T(2,128)(2,1)}), bf16[8,2,256]{2,1,0:T(2,128)(2,1)S(1)}, u32[]{:S(2)}, u32[]{:S(2)}) async-start(bf16[8,2,256]{2,1,0:T(2,128)(2,1)} %reshape.178), calls=%async_computation | async-start | bytes 16384 | tf_op jit(solution)/shard_map/all_to_all | solution.py:105
  85.1 1.4 %copy-start.2 = (bf16[8,64,128]{2,1,0:T(8,128)(2,1)S(1)}, bf16[8,64,128]{2,1,0:T(8,128)(2,1)}, u32[]{:S(2)}) copy-start(bf16[8,64,128]{2,1,0:T(8,128)(2,1)} %param.12) | copy-start | bytes 393220
where the time goes:
time: 88.6 us; the launch traced here: 88.1 us
  blocking collectives  63.4 us (72%)
  other arithmetic  7.06 us (8%)
  local copies, waits for them, and re-layouts  5.95 us (7%)
  starting transfers between devices  5.47 us (6%)
  matrix products  5.34 us (6%)
    all_gather x1, blocking collectives, on_device(): bias_all = lax.all_gather(bias_here, 'dap', axis=1, tiled=True)  32.3 us
    all_gather x1, blocking collectives, on_device(): piece = lax.all_gather(right_rows, 'dap', axis=1, tiled=True)  31.1 us
    all_to_all x1, starting transfers between devices, on_device(): lax.all_to_all(left_rows, 'dap', split_axis=0, concat_axis=1, tiled=True)  5.47 us
    unnamed x17, local copies, waits for them, and re-layouts  2.54 us
    reduce_sum x3, other arithmetic, standardize_features(): spread = jnp.mean(center * center, axis=-1, keepdims=True)  2.46 us
    reduce_sum x2, other arithmetic, standardize_features(): center = x - jnp.mean(x, axis=-1, keepdims=True)  2.16 us
  transfers between devices with their start and end apart: 1, of which 0 were waited for; matrix products, arithmetic and copies ran while one was open for 0% of the time, Pallas kernels for 0%

commit v1 on v0

--- a/solution.py
+++ b/solution.py
@@ -102,7 +102,10 @@
         .astype(jnp.bfloat16)
         .reshape(every_amino_line, device_aligned_lines * width)
     )
-    left_full = lax.all_to_all(left_rows, "dap", split_axis=0, concat_axis=1, tiled=True)
+    left_full = jnp.concatenate(
+        lax.all_to_all(jnp.stack(jnp.split(left_rows, lax.axis_size("dap"), axis=0)), "dap", 0, 0),
+        axis=1,
+    )
     piece = lax.all_gather(right_rows, "dap", axis=1, tiled=True)
     columns = piece.shape[1]
     left_part = left_full.reshape(res_here, columns // width, width)

time: 88.6 us -> 89.2 us (level)
    unnamed x17 -> x24, local copies, waits for them, and re-layouts: 2.54 us -> 2.6 us
where the time goes in v1:
time: 89.2 us; the launch traced here: 88.7 us
  blocking collectives  63.4 us (71%)
  other arithmetic  7.06 us (8%)
  local copies, waits for them, and re-layouts  6.56 us (7%)
  starting transfers between devices  5.47 us (6%)
  matrix products  5.34 us (6%)
  between operations  0.9 us (1%)
    all_gather x1, blocking collectives, on_device(): bias_all = lax.all_gather(bias_here, 'dap', axis=1, tiled=True)  32.3 us
    all_gather x1, blocking collectives, on_device(): piece = lax.all_gather(right_rows, 'dap', axis=1, tiled=True)  31.1 us
    all_to_all x1, starting transfers between devices, on_device(): lax.all_to_all(jnp.stack(jnp.split(left_rows, lax.axis_size('dap'), axis=...  5.47 us
    unnamed x24, local copies, waits for them, and re-layouts  2.6 us
    reduce_sum x3, other arithmetic, standardize_features(): spread = jnp.mean(center * center, axis=-1, keepdims=True)  2.46 us
    reduce_sum x2, other arithmetic, standardize_features(): center = x - jnp.mean(x, axis=-1, keepdims=True)  2.16 us
  transfers between devices with their start and end apart: 1, of which 0 were waited for; matrix products, arithmetic and copies ran while one was open for 0% of the time, Pallas kernels for 0%

profile of v1, /device:TPU:0, one launch (start us, length us, event | category | flops | bytes accessed | tf_op | source)
XLA Modules:
  0.0 88.7 jit_solution(8231396437722377889)
XLA Ops:
  0.7 0.8 dynamic_slice.12
  1.4 0.7 broadcast_subtract_fusion
  2.2 0.7 compare_convert_fusion
  2.9 0.9 %convert_reduce_fusion = f32[2,64]{1,0:T(2,128)S(1)} fusion(bf16[2,64,256]{2,1,0:T(8,128)(2,1)} %param.11), kind=kLoop, calls=%fused_computation.35 | loop fusion | flops 65408 | bytes 66048 | tf_op jit(solution)/shard_map/reduce_sum | solution.py:11
  3.8 1.0 %fusion.24 = f32[2,64]{1,0:T(2,128)S(1)} fusion(bf16[2,64,256]{2,1,0:T(8,128)(2,1)} %param.11, f32[2,64]{1,0:T(2,128)S(1)} %broadcast_multiply_fusion.3), kind=kLoop, calls=%fused_computation.42 | loop fusion | flops 130944 | bytes 66560 | tf_op jit(solution)/shard_map/reduce_sum | solution.py:12
  4.9 0.8 slice_bitcast_fusion.5
  5.6 1.2 %fusion.19 = f32[8,64]{1,0:T(8,128)S(1)} fusion(bf16[8,64,128]{2,1,0:T(8,128)(2,1)} %param.12, f32[128]{0:T(128)S(1)} %get-tuple-element.15, f32[8,64]{1,0:T(8,128)S(1)} %compare_convert_fusion, f32[128]{0:T(128)S(1)} %get-tuple-element.14, f32[8,64]{1,0:T(8,128)S(1)} %broadcast_subtract_fusion), kind=kLoop, calls=%fused_computation.33 | loop fusion | flops 392704 | bytes 138240 | tf_op jit(solution)/shard_map/reduce_sum | solution.py:11
  6.9 1.3 %multiply_reduce_fusion = f32[8,64]{1,0:T(8,128)S(1)} fusion(bf16[8,64,128]{2,1,0:T(8,128)(2,1)} %param.12, f32[8,64]{1,0:T(8,128)S(1)} %broadcast_multiply_fusion.1, f32[128]{0:T(128)S(1)} %get-tuple-element.15, f32[8,64]{1,0:T(8,128)S(1)} %compare_convert_fusion, f32[128]{0:T(128)S(1)} %get-tuple-element.14, f32[8,64]{1,0:T(8,128)S(1)} %broadcast_subtract_fusion), kind=kLoop, calls=%fused_computation.30 | loop fusion | flops 523776 | bytes 140288 | tf_op jit(solution)/shard_map/reduce_sum | solution.py:12
  8.2 0.7 convert_element_type.94
  8.9 1.4 %fusion.10 = bf16[8,8,64]{2,0,1:T(8,128)(2,1)S(1)} fusion(bf16[8,64,128]{2,1,0:T(8,128)(2,1)} %param.12, f32[8,64]{1,0:T(8,128)S(1)} %add_rsqrt_fusion, f32[8,64]{1,0:T(8,128)S(1)} %broadcast_multiply_fusion.1, f32[128]{0:T(128)S(1)} %get-tuple-element.15, f32[8,64]{1,0:T(8,128)S(1)} %compare_convert_fusion, f32[128]{0:T(128)S(1)} %get-tuple-element.14, ...), kind=kOutput, calls=%fused_computation.17 | convolution fusion | flops 1576960 | bytes 150528 | tf_op jit(solution)/shard_map/ijc,ch->hij/dot_general | solution.py:46
  10.2 32.3 %all_gather.6 = bf16[8,64,64]{2,0,1:T(8,128)(2,1)S(1)} all-gather(bf16[8,8,64]{2,0,1:T(8,128)(2,1)S(1)} %fusion.10), channel_id=1, replica_groups=mesh['cplx'=4,'dap'=8] {'dap'}, dimensions={1}, use_global_device_ids=true | all-gather | bytes 73728 | tf_op jit(solution)/shard_map/all_gather | solution.py:49
  42.7 1.2 %copy.26 = bf16[256,1024]{0,1:T(8,128)(2,1)S(1)} copy(bf16[256,1024]{1,0:T(8,128)(2,1)} %param.17) | data formatting | bytes 1048576 | tf_op args[6]
  44.0 0.4 fusion.50
  44.4 0.3 fusion.3
  44.9 0.2 fusion.7
  45.1 0.5 copy-done.4
  45.6 0.3 convert_reduce_fusion.1
  47.2 0.7 reshape.189
  47.9 5.5 %all-to-all-start = ((bf16[8,2,256]{2,1,0:T(2,128)(2,1)}), bf16[8,2,256]{2,1,0:T(2,128)(2,1)S(1)}, u32[]{:S(2)}, u32[]{:S(2)}) async-start(bf16[8,2,256]{2,1,0:T(2,128)(2,1)} %reshape.189), calls=%async_computation | async-start | bytes 16384 | tf_op jit(solution)/shard_map/all_to_all | solution.py:106
  53.3 0.3 convolution_add_fusion.2
  53.8 31.1 %all_gather.7 = bf16[64,512]{0,1:T(8,128)(2,1)S(1)} all-gather(bf16[64,64]{0,1:T(8,128)(2,1)S(1)} %bitcast.83), channel_id=1, replica_groups=mesh['cplx'=4,'dap'=8] {'dap'}, dimensions={1}, use_global_device_ids=true | all-gather | bytes 73728 | tf_op jit(solution)/shard_map/all_gather | solution.py:109
  85.0 0.7 convert_bitcast_fusion
  85.8 1.4 %copy.40 = bf16[8,64,32,32]{1,3,2,0:T(8,128)(2,1)S(1)} copy(bf16[8,64,32,32]{1,2,0,3:T(8,128)(2,1)S(1)} %convert_bitcast_fusion) | data formatting | bytes 2097152 | tf_op jit(solution)/shard_map/convert_element_type | solution.py:114
  87.2 1.6 %fusion.8 = bf16[8,64,128]{2,1,0:T(8,128)(2,1)} fusion(bf16[8,64,1024]{1,2,0:T(8,128)(2,1)S(1)} %bitcast.80, bf16[1024,128]{1,0:T(8,128)(2,1)S(1)} %copy-done, bf16[8,64,128]{2,1,0:T(8,128)(2,1)S(1)} %copy-done.2, f32[8,64]{1,0:T(8,128)S(1)} %convolution_add_fusion.2, f32[8,64]{1,0:T(8,128)S(1)} %broadcast_multiply_fusion, f32[128]{0:T(128)S(1)} %get-tuple-element.15, ...), kind=kOutput, calls=%fused_computation.12 | convolution fusion | flops 134807552 | bytes 1582080 | tf_op jit(solution)/shard_map/ijk,kz->ijz/dot_general | solution.py:116
  (49 shorter events, 1.9 us)
Async XLA Ops:
  0.6 86.5 %copy-start = (bf16[1024,128]{1,0:T(8,128)(2,1)S(1)}, bf16[1024,128]{1,0:T(8,128)(2,1)}, u32[]{:S(2)}) copy-start(bf16[1024,128]{1,0:T(8,128)(2,1)} %param.21) | copy-start | bytes 786436
  0.6 43.3 %copy-start.1 = (bf16[2,64,256]{2,1,0:T(8,128)(2,1)S(1)}, bf16[2,64,256]{2,1,0:T(8,128)(2,1)}, u32[]{:S(2)}) copy-start(bf16[2,64,256]{2,1,0:T(8,128)(2,1)} %param.11) | copy-start | bytes 196612
  44.7 0.9 %copy-start.4 = (bf16[256,256]{1,0:T(8,128)(2,1)S(1)}, bf16[256,256]{1,0:T(8,128)(2,1)}, u32[]{:S(2)}) copy-start(bf16[256,256]{1,0:T(8,128)(2,1)} %param.18) | copy-start | bytes 393220
  44.8 1.2 %copy-start.5 = (bf16[256,64]{0,1:T(8,128)(2,1)S(1)}, bf16[256,64]{0,1:T(8,128)(2,1)}, u32[]{:S(2)}) copy-start(bf16[256,64]{0,1:T(8,128)(2,1)} %param.20) | copy-start | bytes 98308
  44.8 8.8 %copy-start.6 = (s32[64]{0:T(128)S(1)}, s32[64]{0:T(128)}, u32[]{:S(2)}) copy-start(s32[64]{0:T(128)} %param.14) | copy-start | bytes 772
  45.9 41.3 %copy-start.3 = (bf16[2,64,256]{2,1,0:T(8,128)(2,1)}, bf16[2,64,256]{2,1,0:T(8,128)(2,1)S(1)}, u32[]{:S(2)}) copy-start(bf16[2,64,256]{2,1,0:T(8,128)(2,1)S(1)} %get-tuple-element.19) | copy-start | bytes 196612
  47.9 37.0 %all-to-all-start = ((bf16[8,2,256]{2,1,0:T(2,128)(2,1)}), bf16[8,2,256]{2,1,0:T(2,128)(2,1)S(1)}, u32[]{:S(2)}, u32[]{:S(2)}) async-start(bf16[8,2,256]{2,1,0:T(2,128)(2,1)} %reshape.189), calls=%async_computation | async-start | bytes 16384 | tf_op jit(solution)/shard_map/all_to_all | solution.py:106
  85.8 1.4 %copy-start.2 = (bf16[8,64,128]{2,1,0:T(8,128)(2,1)S(1)}, bf16[8,64,128]{2,1,0:T(8,128)(2,1)}, u32[]{:S(2)}) copy-start(bf16[8,64,128]{2,1,0:T(8,128)(2,1)} %param.12) | copy-start | bytes 393220
